TPU v7x, 32 devices: a whole 2x2x4 slice. The times are simulated.
32 devices in a mesh: rows: 8 (over z, y), cols: 4 (over x, core).
Axes of the slice: x: 2, y: 2, z: 4, core: 2. Of those that a mesh axis runs over, the one named last changes fastest.
Arguments:
- sketches: bfloat16 [2048, 16384], P('rows', 'cols'), may hold values from -6 to 6, as said below
- start_basis: bfloat16 [16384, 256], P('cols'), may hold values from -6 to 6
- shrink_index: int32 [1], replicated, may hold values from 64 to 191
Outputs:
- shrunk: float32 [256, 16384], P('rows', 'cols')
Inputs may be any that keep to these rules, and one draw needn't show every extreme that they name: `sketches`: real entries.
All inputs are finite; a program needn't handle non-finite values.
Results may differ from a plain program's by a relative error of at most 0.0028.
Values may be sent and summed in bfloat16 or wider, within the bound.
A program may use at most 64 MiB of HBM per device.

v0:
```python
import jax
import jax.numpy as jnp
from jax import lax
from jax.sharding import PartitionSpec as P

ITERS = 3


def project(sketches, basis_bf):
    partial_product = jnp.dot(sketches, basis_bf, preferred_element_type=jnp.float32)
    return lax.psum(partial_product, "cols")


def orthonormal(images, gram_total):
    lower_factor = jnp.linalg.cholesky(gram_total)
    return jax.scipy.linalg.solve_triangular(lower_factor, images.T, lower=True).T


def body(sketches, start_basis, shrink_index):
    basis_bf = start_basis
    basis = start_basis.astype(jnp.float32)
    for loop_index in range(ITERS):
        projected_bf = project(sketches, basis_bf).astype(jnp.bfloat16)
        local_images = jnp.einsum(
            "lw,lk->wk", sketches, projected_bf, preferred_element_type=jnp.float32
        )
        images = lax.psum(local_images, "rows")
        gram_total = lax.psum(jnp.dot(images.T, images, precision=lax.Precision.HIGHEST), "cols")
        basis = orthonormal(images, gram_total)
        basis_bf = basis.astype(jnp.bfloat16)
    projected = project(sketches, basis_bf)
    energy = lax.psum(jnp.sum(projected * projected, axis=0), "rows")
    ordered = jnp.sort(energy)[::-1]
    threshold = lax.dynamic_index_in_dim(ordered, shrink_index[0], 0, keepdims=False)
    factor = jnp.sqrt(jnp.maximum(energy - threshold, 0.25 * threshold))
    owned_rows = basis.shape[1] // lax.axis_size("rows")
    offset = lax.axis_index("rows") * owned_rows
    columns = lax.dynamic_slice_in_dim(basis, offset, owned_rows, 1)
    scaled = columns * lax.dynamic_slice_in_dim(factor, offset, owned_rows, 0)[None, :]
    return scaled.T


def solution(mesh):
    return jax.shard_map(
        body,
        mesh=mesh,
        in_specs=(P("rows", "cols"), P("cols", None), P()),
        out_specs=P("rows", "cols"),
        check_vma=False,
    )
```

profile of v0, /device:TPU:0, one launch (start us, length us, event | category | flops | bytes accessed | tf_op | source)
XLA Modules:
  0.0 932.8 jit_solution(5308531713813557644)
XLA Ops:
  10.4 16.3 %all-reduce.25 = bf16[256,256]{1,0:T(8,128)(2,1)S(1)} all-reduce(f32[256,256]{1,0:T(8,128)S(1)} %fusion.53), channel_id=1, replica_groups=mesh['rows'=8,'cols'=4] {'cols'}, use_global_device_ids=true, to_apply=%region_0.0 | all-reduce | flops 65536 | bytes 393216 | tf_op jit(solution)/shard_map/psum | solution.py:11
  29.5 157.0 %all-reduce.12.cloned.1.call-done = f32[4096,256]{0,1:T(8,128)} async-done(((f32[4096,256]{0,1:T(8,128)}), f32[4096,256]{0,1:T(8,128)}) %all-reduce.12.cloned.1.call-update) | async-done | bytes 4194320 | tf_op jit(solution)/shard_map/psum | solution.py:27
  186.5 7.7 fusion.54
  194.7 30.9 %all-reduce.14.cloned.1.call-done = f32[256,256]{0,1:T(8,128)} async-done(((f32[256,256]{0,1:T(8,128)}), f32[256,256]{0,1:T(8,128)}) %all-reduce.14.cloned.1.call-update) | async-done | bytes 262160 | tf_op jit(solution)/shard_map/psum | solution.py:28
  227.7 11.7 %cholesky.172 = f32[128,128]{1,0:T(8,128)S(1)} custom-call(f32[128,128]{1,0:T(8,128)S(1)} %cholesky.270), custom_call_target="Cholesky" | custom-call | tf_op jit(solution)/shard_map/jit(cholesky)/cholesky | solution.py:15
  239.5 9.8 %custom-call.15 = f32[1,128,128]{1,2,0:T(8,128)S(1)} custom-call(f32[1,128,128]{2,1,0:T(8,128)S(1)} %get-tuple-element.74), custom_call_target="InvertDiagBlocksLowerTriangular" | custom-call | tf_op jit(solution)/shard_map/jit(cholesky)/cholesky | solution.py:15
  249.8 11.7 %cholesky.189 = f32[128,128]{1,0:T(8,128)S(1)} custom-call(f32[128,128]{1,0:T(8,128)S(1)} %convolution_subtract_fusion.5), custom_call_target="Cholesky" | custom-call | tf_op jit(solution)/shard_map/jit(cholesky)/cholesky | solution.py:15
  267.7 19.7 %custom-call.16 = f32[2,128,128]{1,2,0:T(8,128)S(1)} custom-call(f32[2,128,128]{2,1,0:T(8,128)S(1)} %get-tuple-element.30), custom_call_target="InvertDiagBlocksLowerTriangular" | custom-call | tf_op jit(solution)/shard_map/jit(_solve_triangular)/triangular_solve | solution.py:16
  295.9 13.5 %all-reduce.26 = bf16[256,256]{0,1:T(8,128)(2,1)S(1)} all-reduce(f32[256,256]{0,1:T(8,128)S(1)} %fusion.14), channel_id=1, replica_groups=mesh['rows'=8,'cols'=4] {'cols'}, use_global_device_ids=true, to_apply=%region_7.0 | all-reduce | flops 65536 | bytes 393216 | tf_op jit(solution)/shard_map/psum | solution.py:11
  312.1 156.6 %all-reduce.16.cloned.1.call-done = f32[4096,256]{0,1:T(8,128)} async-done(((f32[4096,256]{0,1:T(8,128)}), f32[4096,256]{0,1:T(8,128)}) %all-reduce.16.cloned.1.call-update) | async-done | bytes 4194320 | tf_op jit(solution)/shard_map/psum | solution.py:27
  476.9 31.0 %all-reduce.18.cloned.1.call-done = f32[256,256]{0,1:T(8,128)} async-done(((f32[256,256]{0,1:T(8,128)}), f32[256,256]{0,1:T(8,128)}) %all-reduce.18.cloned.1.call-update) | async-done | bytes 262160 | tf_op jit(solution)/shard_map/psum | solution.py:28
  509.9 11.7 %cholesky.206 = f32[128,128]{1,0:T(8,128)S(1)} custom-call(f32[128,128]{1,0:T(8,128)S(1)} %cholesky.273), custom_call_target="Cholesky" | custom-call | tf_op jit(solution)/shard_map/jit(cholesky)/cholesky | solution.py:15
  521.7 9.8 %custom-call.17 = f32[1,128,128]{1,2,0:T(8,128)S(1)} custom-call(f32[1,128,128]{2,1,0:T(8,128)S(1)} %get-tuple-element.70), custom_call_target="InvertDiagBlocksLowerTriangular" | custom-call | tf_op jit(solution)/shard_map/jit(cholesky)/cholesky | solution.py:15
  532.0 11.7 %cholesky.223 = f32[128,128]{1,0:T(8,128)S(1)} custom-call(f32[128,128]{1,0:T(8,128)S(1)} %convolution_subtract_fusion.4), custom_call_target="Cholesky" | custom-call | tf_op jit(solution)/shard_map/jit(cholesky)/cholesky | solution.py:15
  550.5 19.7 %custom-call.18 = f32[2,128,128]{1,2,0:T(8,128)S(1)} custom-call(f32[2,128,128]{2,1,0:T(8,128)S(1)} %get-tuple-element.31), custom_call_target="InvertDiagBlocksLowerTriangular" | custom-call | tf_op jit(solution)/shard_map/jit(_solve_triangular)/triangular_solve | solution.py:16
  578.7 13.5 %all-reduce.27 = bf16[256,256]{0,1:T(8,128)(2,1)S(1)} all-reduce(f32[256,256]{0,1:T(8,128)S(1)} %fusion.15), channel_id=1, replica_groups=mesh['rows'=8,'cols'=4] {'cols'}, use_global_device_ids=true, to_apply=%region_10.0 | all-reduce | flops 65536 | bytes 393216 | tf_op jit(solution)/shard_map/psum | solution.py:11
  594.9 156.5 %all-reduce.20.cloned.1.call-done = f32[4096,256]{0,1:T(8,128)} async-done(((f32[4096,256]{0,1:T(8,128)}), f32[4096,256]{0,1:T(8,128)}) %all-reduce.20.cloned.1.call-update) | async-done | bytes 4194320 | tf_op jit(solution)/shard_map/psum | solution.py:27
  759.4 31.2 %all-reduce.22.cloned.1.call-done = f32[256,256]{0,1:T(8,128)} async-done(((f32[256,256]{0,1:T(8,128)}), f32[256,256]{0,1:T(8,128)}) %all-reduce.22.cloned.1.call-update) | async-done | bytes 262160 | tf_op jit(solution)/shard_map/psum | solution.py:28
  792.7 11.7 %cholesky.240 = f32[128,128]{1,0:T(8,128)S(1)} custom-call(f32[128,128]{1,0:T(8,128)S(1)} %cholesky.276), custom_call_target="Cholesky" | custom-call | tf_op jit(solution)/shard_map/jit(cholesky)/cholesky | solution.py:15
  804.5 9.8 %custom-call.19 = f32[1,128,128]{1,2,0:T(8,128)S(1)} custom-call(f32[1,128,128]{2,1,0:T(8,128)S(1)} %get-tuple-element.66), custom_call_target="InvertDiagBlocksLowerTriangular" | custom-call | tf_op jit(solution)/shard_map/jit(cholesky)/cholesky | solution.py:15
  814.8 11.7 %cholesky.257 = f32[128,128]{1,0:T(8,128)S(1)} custom-call(f32[128,128]{1,0:T(8,128)S(1)} %convolution_subtract_fusion.3), custom_call_target="Cholesky" | custom-call | tf_op jit(solution)/shard_map/jit(cholesky)/cholesky | solution.py:15
  833.3 19.7 %custom-call.20 = f32[2,128,128]{1,2,0:T(8,128)S(1)} custom-call(f32[2,128,128]{2,1,0:T(8,128)S(1)} %get-tuple-element.32), custom_call_target="InvertDiagBlocksLowerTriangular" | custom-call | tf_op jit(solution)/shard_map/jit(_solve_triangular)/triangular_solve | solution.py:16
  864.0 31.8 %all-reduce.24.cloned.1.call-done = f32[256,256]{0,1:T(8,128)} async-done(((f32[256,256]{0,1:T(8,128)}), f32[256,256]{0,1:T(8,128)}) %all-reduce.24.cloned.1.call-update) | async-done | bytes 262160 | tf_op jit(solution)/shard_map/psum | solution.py:11
  896.9 21.4 %psum.87 = f32[256]{0:T(256)S(1)} all-reduce(f32[256]{0:T(256)S(1)} %multiply_reduce_fusion), channel_id=1, replica_groups=mesh['rows'=8,'cols'=4] {'rows'}, use_global_device_ids=true, to_apply=%region_15.18 | all-reduce | flops 256 | bytes 2048 | tf_op jit(solution)/shard_map/psum | solution.py:32
  (110 shorter events, 99.1 us)
Async XLA Ops:
  6.5 1.6 copy-start
  6.5 179.9 %all-reduce.12.cloned.1.call-start = ((), (), s32[]{:S(2)}) async-start(), calls=%async_computation | async-start | bytes 8388608 | tf_op jit(solution)/shard_map/psum | solution.py:27
  29.4 196.2 %all-reduce.14.cloned.1.call-start = ((), (), s32[]{:S(2)}) async-start(), calls=%async_computation.1 | async-start | bytes 524288 | tf_op jit(solution)/shard_map/psum | solution.py:28
  194.2 274.5 %all-reduce.16.cloned.1.call-start = ((), (), s32[]{:S(2)}) async-start(), calls=%async_computation.2 | async-start | bytes 8388608 | tf_op jit(solution)/shard_map/psum | solution.py:27
  287.4 3.7 copy-start.1
  312.1 195.8 %all-reduce.18.cloned.1.call-start = ((), (), s32[]{:S(2)}) async-start(), calls=%async_computation.3 | async-start | bytes 524288 | tf_op jit(solution)/shard_map/psum | solution.py:28
  476.4 275.0 %all-reduce.20.cloned.1.call-start = ((), (), s32[]{:S(2)}) async-start(), calls=%async_computation.4 | async-start | bytes 8388608 | tf_op jit(solution)/shard_map/psum | solution.py:27
  570.2 3.7 copy-start.3
  594.9 195.7 %all-reduce.22.cloned.1.call-start = ((), (), s32[]{:S(2)}) async-start(), calls=%async_computation.5 | async-start | bytes 524288 | tf_op jit(solution)/shard_map/psum | solution.py:28
  759.2 136.6 %all-reduce.24.cloned.1.call-start = ((), (), s32[]{:S(2)}) async-start(), calls=%async_computation.6 | async-start | bytes 524288 | tf_op jit(solution)/shard_map/psum | solution.py:11
  853.0 3.7 copy-start.2
  856.7 3.9 copy-start.4
  860.6 1.3 copy-start.5
Sparse Core Ops, SparseCore 0:
  29.6 156.8 all-reduce.11
  194.3 31.2 all-reduce.13
  312.2 156.4 all-reduce.15
  476.5 31.2 all-reduce.17
  595.0 156.4 all-reduce.19
  759.3 31.2 all-reduce.21
  863.5 32.2 all-reduce.23
where the time goes:
time: 938 us; the launch traced here: 933 us
  waiting for transfers between devices  595 us (63%)
  other arithmetic  172 us (18%)
  blocking collectives  64.6 us (7%)
  matrix products  60.7 us (6%)
  between operations  19.5 us (2%)
  local copies, waits for them, and re-layouts  18.7 us (2%)
    psum x3, waiting for transfers between devices, body(): images = lax.psum(local_images, 'rows')  470 us
    another operation x20, other arithmetic, orthonormal(): lower_factor = jnp.linalg.cholesky(gram_total)  103 us
    psum x3, waiting for transfers between devices, body(): lax.psum(jnp.dot(images.T, images, precision=lax.Precision.HIGHEST), 'cols')  93 us
    another operation x7, other arithmetic, orthonormal(): jax.scipy.linalg.solve_triangular(lower_factor, images.T, lower=True)  59.1 us
    psum x3, blocking collectives, project(): return lax.psum(partial_product, 'cols')  43.3 us
    psum x1, waiting for transfers between devices, project(): return lax.psum(partial_product, 'cols')  31.8 us
    dot_general x3, matrix products, body(): jnp.dot(images.T, images, precision=lax.Precision.HIGHEST)  23.1 us
    another operation x9, matrix products, orthonormal(): jax.scipy.linalg.solve_triangular(lower_factor, images.T, lower=True)  22.6 us
  transfers between devices with their start and end apart: 7, of which 7 were waited for; matrix products, arithmetic and copies ran while one was open for 0% of the time, Pallas kernels for 0%

commit v1 on v0

--- a/solution.py
+++ b/solution.py
@@ -25,7 +25,9 @@
             "lw,lk->wk", sketches, projected_bf, preferred_element_type=jnp.float32
         )
         images = lax.psum(local_images, "rows")
-        gram_total = lax.psum(jnp.dot(images.T, images, precision=lax.Precision.HIGHEST), "cols")
+        x = jnp.dot(images.T, images, precision=lax.Precision.HIGHEST)
+        blocks = lax.all_gather(x, "cols")
+        gram_total = jnp.sum(blocks, axis=0)
         basis = orthonormal(images, gram_total)
         basis_bf = basis.astype(jnp.bfloat16)
     projected = project(sketches, basis_bf)

time: 938 us -> 891 us (0.950)
  waiting for transfers between devices: 595 us -> 550 us
    psum x3 -> x0, waiting for transfers between devices: 93 us -> none  [body(): lax.psum(jnp.dot(images.T, images, precision=lax.Precision.HIGHEST), 'cols')]
    all_gather x0 -> x3, waiting for transfers between devices: none -> 46.3 us  [body(): blocks = lax.all_gather(x, 'cols')]
where the time goes in v1:
time: 891 us; the launch traced here: 886 us
  waiting for transfers between devices  550 us (62%)
  other arithmetic  173 us (19%)
  blocking collectives  64.9 us (7%)
  matrix products  60.7 us (7%)
  between operations  19.5 us (2%)
  local copies, waits for them, and re-layouts  15.9 us (2%)
    psum x3, waiting for transfers between devices, body(): images = lax.psum(local_images, 'rows')  472 us
    another operation x20, other arithmetic, orthonormal(): lower_factor = jnp.linalg.cholesky(gram_total)  103 us
    another operation x7, other arithmetic, orthonormal(): jax.scipy.linalg.solve_triangular(lower_factor, images.T, lower=True)  59.1 us
    all_gather x3, waiting for transfers between devices, body(): blocks = lax.all_gather(x, 'cols')  46.3 us
    psum x3, blocking collectives, project(): return lax.psum(partial_product, 'cols')  43.5 us
    psum x1, waiting for transfers between devices, project(): return lax.psum(partial_product, 'cols')  31.8 us
    dot_general x3, matrix products, body(): x = jnp.dot(images.T, images, precision=lax.Precision.HIGHEST)  23.1 us
    another operation x9, matrix products, orthonormal(): jax.scipy.linalg.solve_triangular(lower_factor, images.T, lower=True)  22.6 us
  transfers between devices with their start and end apart: 7, of which 7 were waited for; matrix products, arithmetic and copies ran while one was open for 0% of the time, Pallas kernels for 0%

profile of v1, /device:TPU:0, one launch (start us, length us, event | category | flops | bytes accessed | tf_op | source)
XLA Modules:
  0.0 886.2 jit_solution(11373086289368153035)
XLA Ops:
  10.4 16.3 %all-reduce.16 = bf16[256,256]{1,0:T(8,128)(2,1)S(1)} all-reduce(f32[256,256]{1,0:T(8,128)S(1)} %fusion.53), channel_id=1, replica_groups=mesh['rows'=8,'cols'=4] {'cols'}, use_global_device_ids=true, to_apply=%region_0.0 | all-reduce | flops 65536 | bytes 393216 | tf_op jit(solution)/shard_map/psum | solution.py:11
  29.5 157.0 %all-reduce.9.cloned.1.call-done = f32[4096,256]{0,1:T(8,128)} async-done(((f32[4096,256]{0,1:T(8,128)}), f32[4096,256]{0,1:T(8,128)}) %all-reduce.9.cloned.1.call-update) | async-done | bytes 4194320 | tf_op jit(solution)/shard_map/psum | solution.py:27
  186.5 7.7 fusion.54
  194.7 15.3 %all-gather.7.cloned.1.call-done = f32[1024,256]{1,0:T(8,128)} async-done(((f32[256,256]{1,0:T(8,128)}), f32[1024,256]{1,0:T(8,128)}) %all-gather.7.cloned.1.call-update) | async-done | bytes 1048592 | tf_op jit(solution)/shard_map/all_gather | solution.py:29
  211.6 11.7 %cholesky.172 = f32[128,128]{1,0:T(8,128)S(1)} custom-call(f32[128,128]{1,0:T(8,128)S(1)} %cholesky.270), custom_call_target="Cholesky" | custom-call | tf_op jit(solution)/shard_map/jit(cholesky)/cholesky | solution.py:15
  223.3 9.8 %custom-call.15 = f32[1,128,128]{1,2,0:T(8,128)S(1)} custom-call(f32[1,128,128]{2,1,0:T(8,128)S(1)} %get-tuple-element.74), custom_call_target="InvertDiagBlocksLowerTriangular" | custom-call | tf_op jit(solution)/shard_map/jit(cholesky)/cholesky | solution.py:15
  233.6 11.7 %cholesky.189 = f32[128,128]{1,0:T(8,128)S(1)} custom-call(f32[128,128]{1,0:T(8,128)S(1)} %convolution_subtract_fusion.5), custom_call_target="Cholesky" | custom-call | tf_op jit(solution)/shard_map/jit(cholesky)/cholesky | solution.py:15
  251.6 19.7 %custom-call.16 = f32[2,128,128]{1,2,0:T(8,128)S(1)} custom-call(f32[2,128,128]{2,1,0:T(8,128)S(1)} %get-tuple-element.30), custom_call_target="InvertDiagBlocksLowerTriangular" | custom-call | tf_op jit(solution)/shard_map/jit(_solve_triangular)/triangular_solve | solution.py:16
  279.7 13.6 %all-reduce.17 = bf16[256,256]{0,1:T(8,128)(2,1)S(1)} all-reduce(f32[256,256]{0,1:T(8,128)S(1)} %fusion.14), channel_id=1, replica_groups=mesh['rows'=8,'cols'=4] {'cols'}, use_global_device_ids=true, to_apply=%region_7.0 | all-reduce | flops 65536 | bytes 393216 | tf_op jit(solution)/shard_map/psum | solution.py:11
  296.1 157.4 %all-reduce.11.cloned.1.call-done = f32[4096,256]{0,1:T(8,128)} async-done(((f32[4096,256]{0,1:T(8,128)}), f32[4096,256]{0,1:T(8,128)}) %all-reduce.11.cloned.1.call-update) | async-done | bytes 4194320 | tf_op jit(solution)/shard_map/psum | solution.py:27
  461.6 15.4 %all-gather.9.cloned.1.call-done = f32[1024,256]{1,0:T(8,128)} async-done(((f32[256,256]{1,0:T(8,128)}), f32[1024,256]{1,0:T(8,128)}) %all-gather.9.cloned.1.call-update) | async-done | bytes 1048592 | tf_op jit(solution)/shard_map/all_gather | solution.py:29
  478.6 11.7 %cholesky.206 = f32[128,128]{1,0:T(8,128)S(1)} custom-call(f32[128,128]{1,0:T(8,128)S(1)} %cholesky.273), custom_call_target="Cholesky" | custom-call | tf_op jit(solution)/shard_map/jit(cholesky)/cholesky | solution.py:15
  490.3 9.8 %custom-call.17 = f32[1,128,128]{1,2,0:T(8,128)S(1)} custom-call(f32[1,128,128]{2,1,0:T(8,128)S(1)} %get-tuple-element.70), custom_call_target="InvertDiagBlocksLowerTriangular" | custom-call | tf_op jit(solution)/shard_map/jit(cholesky)/cholesky | solution.py:15
  500.6 11.7 %cholesky.223 = f32[128,128]{1,0:T(8,128)S(1)} custom-call(f32[128,128]{1,0:T(8,128)S(1)} %convolution_subtract_fusion.4), custom_call_target="Cholesky" | custom-call | tf_op jit(solution)/shard_map/jit(cholesky)/cholesky | solution.py:15
  519.1 19.7 %custom-call.18 = f32[2,128,128]{1,2,0:T(8,128)S(1)} custom-call(f32[2,128,128]{2,1,0:T(8,128)S(1)} %get-tuple-element.31), custom_call_target="InvertDiagBlocksLowerTriangular" | custom-call | tf_op jit(solution)/shard_map/jit(_solve_triangular)/triangular_solve | solution.py:16
  547.3 13.6 %all-reduce.18 = bf16[256,256]{0,1:T(8,128)(2,1)S(1)} all-reduce(f32[256,256]{0,1:T(8,128)S(1)} %fusion.15), channel_id=1, replica_groups=mesh['rows'=8,'cols'=4] {'cols'}, use_global_device_ids=true, to_apply=%region_10.0 | all-reduce | flops 65536 | bytes 393216 | tf_op jit(solution)/shard_map/psum | solution.py:11
  563.7 157.4 %all-reduce.13.cloned.1.call-done = f32[4096,256]{0,1:T(8,128)} async-done(((f32[4096,256]{0,1:T(8,128)}), f32[4096,256]{0,1:T(8,128)}) %all-reduce.13.cloned.1.call-update) | async-done | bytes 4194320 | tf_op jit(solution)/shard_map/psum | solution.py:27
  729.0 15.6 %all-gather.11.cloned.1.call-done = f32[1024,256]{1,0:T(8,128)} async-done(((f32[256,256]{1,0:T(8,128)}), f32[1024,256]{1,0:T(8,128)}) %all-gather.11.cloned.1.call-update) | async-done | bytes 1048592 | tf_op jit(solution)/shard_map/all_gather | solution.py:29
  746.1 11.7 %cholesky.240 = f32[128,128]{1,0:T(8,128)S(1)} custom-call(f32[128,128]{1,0:T(8,128)S(1)} %cholesky.276), custom_call_target="Cholesky" | custom-call | tf_op jit(solution)/shard_map/jit(cholesky)/cholesky | solution.py:15
  757.9 9.8 %custom-call.19 = f32[1,128,128]{1,2,0:T(8,128)S(1)} custom-call(f32[1,128,128]{2,1,0:T(8,128)S(1)} %get-tuple-element.66), custom_call_target="InvertDiagBlocksLowerTriangular" | custom-call | tf_op jit(solution)/shard_map/jit(cholesky)/cholesky | solution.py:15
  768.2 11.7 %cholesky.257 = f32[128,128]{1,0:T(8,128)S(1)} custom-call(f32[128,128]{1,0:T(8,128)S(1)} %convolution_subtract_fusion.3), custom_call_target="Cholesky" | custom-call | tf_op jit(solution)/shard_map/jit(cholesky)/cholesky | solution.py:15
  786.8 19.7 %custom-call.20 = f32[2,128,128]{1,2,0:T(8,128)S(1)} custom-call(f32[2,128,128]{2,1,0:T(8,128)S(1)} %get-tuple-element.32), custom_call_target="InvertDiagBlocksLowerTriangular" | custom-call | tf_op jit(solution)/shard_map/jit(_solve_triangular)/triangular_solve | solution.py:16
  817.5 31.8 %all-reduce.15.cloned.1.call-done = f32[256,256]{0,1:T(8,128)} async-done(((f32[256,256]{0,1:T(8,128)}), f32[256,256]{0,1:T(8,128)}) %all-reduce.15.cloned.1.call-update) | async-done | bytes 262160 | tf_op jit(solution)/shard_map/psum | solution.py:11
  850.3 21.4 %psum.63 = f32[256]{0:T(256)S(1)} all-reduce(f32[256]{0:T(256)S(1)} %multiply_reduce_fusion), channel_id=1, replica_groups=mesh['rows'=8,'cols'=4] {'rows'}, use_global_device_ids=true, to_apply=%region_15.18 | all-reduce | flops 256 | bytes 2048 | tf_op jit(solution)/shard_map/psum | solution.py:34
  (113 shorter events, 97.3 us)
Async XLA Ops:
  6.5 1.6 copy-start
  6.5 179.9 %all-reduce.9.cloned.1.call-start = ((), (), s32[]{:S(2)}) async-start(), calls=%async_computation | async-start | bytes 8388608 | tf_op jit(solution)/shard_map/psum | solution.py:27
  29.4 180.6 %all-gather.7.cloned.1.call-start = ((), (), s32[]{:S(2)}) async-start(), calls=%async_computation.4 | async-start | bytes 1310720 | tf_op jit(solution)/shard_map/all_gather | solution.py:29
  194.2 259.3 %all-reduce.11.cloned.1.call-start = ((), (), s32[]{:S(2)}) async-start(), calls=%async_computation.1 | async-start | bytes 8388608 | tf_op jit(solution)/shard_map/psum | solution.py:27
  271.2 3.7 copy-start.1
  296.1 181.0 %all-gather.9.cloned.1.call-start = ((), (), s32[]{:S(2)}) async-start(), calls=%async_computation.5 | async-start | bytes 1310720 | tf_op jit(solution)/shard_map/all_gather | solution.py:29
  461.2 259.9 %all-reduce.13.cloned.1.call-start = ((), (), s32[]{:S(2)}) async-start(), calls=%async_computation.2 | async-start | bytes 8388608 | tf_op jit(solution)/shard_map/psum | solution.py:27
  538.8 3.7 copy-start.3
  563.6 181.0 %all-gather.11.cloned.1.call-start = ((), (), s32[]{:S(2)}) async-start(), calls=%async_computation.6 | async-start | bytes 1310720 | tf_op jit(solution)/shard_map/all_gather | solution.py:29
  728.8 120.5 %all-reduce.15.cloned.1.call-start = ((), (), s32[]{:S(2)}) async-start(), calls=%async_computation.3 | async-start | bytes 524288 | tf_op jit(solution)/shard_map/psum | solution.py:11
  806.4 3.7 copy-start.2
  810.1 3.9 copy-start.4
  814.0 1.3 copy-start.5
Sparse Core Ops, SparseCore 0:
  29.6 156.8 all-reduce.8
  194.3 15.6 all-gather.6
  296.2 157.2 all-reduce.10
  461.3 15.6 all-gather.8
  563.7 157.2 all-reduce.12
  728.9 15.6 all-gather.10
  816.9 32.2 all-reduce.14
